TPU v7x, 32 devices: a whole 2x2x4 slice. The times are simulated.
32 devices in a mesh: samp: 8 (over z, x), state: 4 (over y, core).
Axes of the slice: x: 2, y: 2, z: 4, core: 2. Of those that a mesh axis runs over, the one named last changes fastest.
Arguments:
- energies: bfloat16 [4096, 131072], P('state', 'samp'), may hold values from -12 to 12
- offsets: float32 [4096, 1024], P('state', 'samp'), may hold values from -250 to 250
- counts: int32 [4096], P('state'), may hold values from 1 to 31745, as said below
- labels: int32 [131072], P('samp'), may hold values from 0 to 4095
Outputs:
- free_energy: float32 [4096], P('state')
- own_log_probability: float32 [131072], P('samp')
Inputs may be any that keep to these rules, and one draw needn't show every extreme that they name: counts[k] is the number of samples n with labels[n] = k; every state has a sample, state 4096 - 1 has exactly one, and state 0 has the most.
All inputs are finite; a program needn't handle non-finite values.
Results may differ from a plain program's by a relative error of at most 0.0003.
Values sent between devices are 32-bit elements; how exact they have to be, the bound alone decides.
A program may use at most 256 MiB of HBM per device.

v0:
```python
import jax
import jax.numpy as jnp
from jax import lax
from jax.sharding import PartitionSpec as P

ITERS = 3


def from_root(value, axis, root):
    mine = lax.axis_index(axis) == root
    return lax.psum(jnp.where(mine, value, jnp.zeros_like(value)), axis)


def local_energy(energies, offsets):
    rows, width = energies.shape
    nblk = offsets.shape[1]
    shaped = energies.astype(jnp.float32).reshape(rows, nblk, width // nblk)
    return (shaped + offsets[:, :, None]).reshape(rows, width)


def sample_denominator(energies, offsets, lead):
    terms = lead[:, None] - local_energy(energies, offsets)
    width = terms.shape[1]
    best = jnp.max(terms, axis=0)
    total = jnp.sum(jnp.exp(terms - best[None, :]), axis=0)
    groups = lax.axis_size("state")
    parts = (
        lax.all_to_all(
            best.reshape(groups, width // groups), "state", split_axis=0, concat_axis=0, tiled=True
        ),
        lax.all_to_all(
            total.reshape(groups, width // groups), "state", split_axis=0, concat_axis=0, tiled=True
        ),
    )
    peak = jnp.max(parts[0], axis=0)
    whole = jnp.sum(parts[1] * jnp.exp(parts[0] - peak[None, :]), axis=0)
    return lax.all_gather(peak + jnp.log(whole), "state", axis=0, tiled=True)


def state_update(energies, offsets, denom):
    terms = -local_energy(energies, offsets) - denom[None, :]
    best = lax.pmax(jnp.max(terms, axis=1), "samp")
    total = lax.psum(jnp.sum(jnp.exp(terms - best[:, None]), axis=1), "samp")
    return -(best + jnp.log(total))


def own_terms_local(energies, offsets, lead, local_label):
    rows, width = energies.shape
    nblk = offsets.shape[1]
    block_size = width // nblk
    span = min(width, max(block_size, 512))
    span = span - span % block_size
    while width % span != 0:
        span = span - block_size
    steps_count = width // span
    row_ids = jnp.arange(rows, dtype=jnp.int32)

    def one(index):
        start = index * span
        part = lax.dynamic_slice_in_dim(energies, start, span, 1).astype(jnp.float32)
        shift = lax.dynamic_slice_in_dim(
            offsets, index * (span // block_size), span // block_size, 1
        )
        energy_part = (
            part.reshape(rows, span // block_size, block_size) + shift[:, :, None]
        ).reshape(rows, span)
        wanted = lax.dynamic_slice_in_dim(local_label, start, span, 0)
        match = row_ids[:, None] == wanted[None, :]
        return jnp.sum(jnp.where(match, lead[:, None] - energy_part, 0.0), axis=0)

    return lax.map(one, jnp.arange(steps_count, dtype=jnp.int32)).reshape(width)


def shards(energies, offsets, counts, labels):
    rows, width = energies.shape
    logc = jnp.log(counts.astype(jnp.float32))
    free = jnp.zeros((rows,), jnp.float32)
    for step in range(ITERS):
        denom = sample_denominator(energies, offsets, logc + free)
        free = state_update(energies, offsets, denom)
    lead = logc + free
    denom = sample_denominator(energies, offsets, lead)
    local_label = labels - lax.axis_index("state") * rows
    picked = own_terms_local(energies, offsets, lead, local_label)
    own = lax.psum(picked, "state") - denom
    anchor_value = from_root(free[0:1], "state", 0)
    return (free - anchor_value[0], own)


def solution(mesh):
    return jax.shard_map(
        shards,
        mesh=mesh,
        in_specs=(P("state", "samp"), P("state", "samp"), P("state"), P("samp")),
        out_specs=(P("state"), P("samp")),
        check_vma=False,
    )
```

profile of v0, /device:TPU:0, one launch (start us, length us, event | category | flops | bytes accessed | tf_op | source)
XLA Modules:
  0.0 765.3 jit_solution(17431815662996339874)
XLA Ops:
  7.9 22.2 %add.48 = f32[1024,128,128]{2,1,0:T(8,128)} broadcast(f32[1024,128]{1,0:T(8,128)} %param.7), dimensions={0,1} | broadcast | bytes 67633152 | tf_op jit(solution)/shard_map/add | solution.py:18
  30.0 74.5 %subtract_reduce_fusion.6 = (f32[16384]{0:T(1024)}, f32[1024,16384]{1,0:T(8,128)}) fusion(f32[1024]{0:T(1024)S(1)} %convert_log_fusion, f32[128,8,128,128]{3,2,1,0:T(8,128)} %bitcast.23, bf16[1024,16384]{1,0:T(8,128)(2,1)} %param.6), kind=kLoop, calls=%fused_computation.21 | loop fusion | flops 67092480 | bytes 167841792 | tf_op jit(solution)/shard_map/reduce_max | solution.py:24
  104.5 4.3 all-to-all-start
  108.8 24.4 %exponential_reduce_fusion.6 = f32[16384]{0:T(1024)} fusion(f32[1024,16384]{1,0:T(8,128)} %get-tuple-element.78, f32[16384]{0:T(1024)} %get-tuple-element.77, f32[1024]{0:T(1024)S(1)} %convert_log_fusion), kind=kLoop, calls=%fused_computation.14 | loop fusion | flops 50315264 | bytes 67244032 | tf_op jit(solution)/shard_map/reduce_sum | solution.py:25
  133.2 3.3 all-to-all-start.1
  136.6 4.1 all-to-all-done.1
  140.7 5.2 all_gather.12
  146.0 21.0 %subtract_reduce_fusion.5 = f32[1024]{0:T(1024)S(1)} fusion(f32[1024,16384]{1,0:T(8,128)} %get-tuple-element.78, f32[16384]{0:T(1024)S(1)} %all_gather.12), kind=kLoop, calls=%fused_computation.20 | loop fusion | flops 50330624 | bytes 67178496 | tf_op jit(solution)/shard_map/reduce_max | solution.py:42
  167.0 22.1 %pmax.21 = f32[1024]{0:T(1024)S(1)} all-reduce(f32[1024]{0:T(1024)S(1)} %subtract_reduce_fusion.5), channel_id=1, replica_groups=mesh['samp'=8,'state'=4] {'samp'}, use_global_device_ids=true, to_apply=%region_5.0 | all-reduce | flops 1024 | bytes 8192 | tf_op jit(solution)/shard_map/pmax | solution.py:42
  189.1 21.4 %exponential_reduce_fusion.5 = f32[1024]{0:T(1024)S(1)} fusion(f32[1024,16384]{1,0:T(8,128)} %get-tuple-element.78, f32[1024]{0:T(1024)S(1)} %pmax.21, f32[16384]{0:T(1024)S(1)} %all_gather.12), kind=kLoop, calls=%fused_computation.13 | loop fusion | flops 67107840 | bytes 67182592 | tf_op jit(solution)/shard_map/reduce_sum | solution.py:43
  210.5 17.1 %psum.35 = f32[1024]{0:T(1024)S(1)} all-reduce(f32[1024]{0:T(1024)S(1)} %exponential_reduce_fusion.5), channel_id=1, replica_groups=mesh['samp'=8,'state'=4] {'samp'}, use_global_device_ids=true, to_apply=%region_7.0 | all-reduce | flops 1024 | bytes 8192 | tf_op jit(solution)/shard_map/psum | solution.py:43
  227.7 21.5 %subtract_reduce_fusion.4 = f32[16384]{0:T(1024)} fusion(f32[1024,16384]{1,0:T(8,128)} %get-tuple-element.78, f32[1024]{0:T(1024)S(1)} %negate_add_fusion.1), kind=kLoop, calls=%fused_computation.19 | loop fusion | flops 33538048 | bytes 67178496 | tf_op jit(solution)/shard_map/reduce_max | solution.py:24
  249.2 3.3 all-to-all-start.2
  252.4 24.4 %exponential_reduce_fusion.4 = f32[16384]{0:T(1024)} fusion(f32[1024,16384]{1,0:T(8,128)} %get-tuple-element.78, f32[16384]{0:T(1024)} %subtract_reduce_fusion.4, f32[1024]{0:T(1024)S(1)} %negate_add_fusion.1), kind=kLoop, calls=%fused_computation.12 | loop fusion | flops 50315264 | bytes 67244032 | tf_op jit(solution)/shard_map/reduce_sum | solution.py:25
  276.9 3.3 all-to-all-start.3
  280.3 4.0 all-to-all-done.3
  284.4 5.2 all_gather.13
  289.6 21.0 %subtract_reduce_fusion.3 = f32[1024]{0:T(1024)S(1)} fusion(f32[1024,16384]{1,0:T(8,128)} %get-tuple-element.78, f32[16384]{0:T(1024)S(1)} %all_gather.13), kind=kLoop, calls=%fused_computation.18 | loop fusion | flops 50330624 | bytes 67178496 | tf_op jit(solution)/shard_map/reduce_max | solution.py:42
  310.7 19.3 %pmax.22 = f32[1024]{0:T(1024)S(1)} all-reduce(f32[1024]{0:T(1024)S(1)} %subtract_reduce_fusion.3), channel_id=1, replica_groups=mesh['samp'=8,'state'=4] {'samp'}, use_global_device_ids=true, to_apply=%region_13.0 | all-reduce | flops 1024 | bytes 8192 | tf_op jit(solution)/shard_map/pmax | solution.py:42
  330.0 21.4 %exponential_reduce_fusion.3 = f32[1024]{0:T(1024)S(1)} fusion(f32[1024,16384]{1,0:T(8,128)} %get-tuple-element.78, f32[1024]{0:T(1024)S(1)} %pmax.22, f32[16384]{0:T(1024)S(1)} %all_gather.13), kind=kLoop, calls=%fused_computation.11 | loop fusion | flops 67107840 | bytes 67182592 | tf_op jit(solution)/shard_map/reduce_sum | solution.py:43
  351.3 17.1 %psum.36 = f32[1024]{0:T(1024)S(1)} all-reduce(f32[1024]{0:T(1024)S(1)} %exponential_reduce_fusion.3), channel_id=1, replica_groups=mesh['samp'=8,'state'=4] {'samp'}, use_global_device_ids=true, to_apply=%region_15.0 | all-reduce | flops 1024 | bytes 8192 | tf_op jit(solution)/shard_map/psum | solution.py:43
  368.5 21.5 %subtract_reduce_fusion.2 = f32[16384]{0:T(1024)} fusion(f32[1024,16384]{1,0:T(8,128)} %get-tuple-element.78, f32[1024]{0:T(1024)S(1)} %negate_add_fusion), kind=kLoop, calls=%fused_computation.17 | loop fusion | flops 33538048 | bytes 67178496 | tf_op jit(solution)/shard_map/reduce_max | solution.py:24
  390.0 3.3 all-to-all-start.4
  393.3 24.4 %exponential_reduce_fusion.2 = f32[16384]{0:T(1024)} fusion(f32[1024,16384]{1,0:T(8,128)} %get-tuple-element.78, f32[16384]{0:T(1024)} %subtract_reduce_fusion.2, f32[1024]{0:T(1024)S(1)} %negate_add_fusion), kind=kLoop, calls=%fused_computation.10 | loop fusion | flops 50315264 | bytes 67244032 | tf_op jit(solution)/shard_map/reduce_sum | solution.py:25
  417.8 3.3 all-to-all-start.5
  421.2 4.0 all-to-all-done.5
  425.3 5.2 all_gather.14
  430.5 21.0 %subtract_reduce_fusion.1 = f32[1024]{0:T(1024)S(1)} fusion(f32[1024,16384]{1,0:T(8,128)} %get-tuple-element.78, f32[16384]{0:T(1024)S(1)} %all_gather.14), kind=kLoop, calls=%fused_computation.16 | loop fusion | flops 50330624 | bytes 67178496 | tf_op jit(solution)/shard_map/reduce_max | solution.py:42
  451.5 19.1 %pmax.23 = f32[1024]{0:T(1024)S(1)} all-reduce(f32[1024]{0:T(1024)S(1)} %subtract_reduce_fusion.1), channel_id=1, replica_groups=mesh['samp'=8,'state'=4] {'samp'}, use_global_device_ids=true, to_apply=%region_21.0 | all-reduce | flops 1024 | bytes 8192 | tf_op jit(solution)/shard_map/pmax | solution.py:42
  470.7 21.4 %exponential_reduce_fusion.1 = f32[1024]{0:T(1024)S(1)} fusion(f32[1024,16384]{1,0:T(8,128)} %get-tuple-element.78, f32[1024]{0:T(1024)S(1)} %pmax.23, f32[16384]{0:T(1024)S(1)} %all_gather.14), kind=kLoop, calls=%fused_computation.9 | loop fusion | flops 67107840 | bytes 67182592 | tf_op jit(solution)/shard_map/reduce_sum | solution.py:43
  492.1 17.1 %psum.37 = f32[1024]{0:T(1024)S(1)} all-reduce(f32[1024]{0:T(1024)S(1)} %exponential_reduce_fusion.1), channel_id=1, replica_groups=mesh['samp'=8,'state'=4] {'samp'}, use_global_device_ids=true, to_apply=%region_23.0 | all-reduce | flops 1024 | bytes 8192 | tf_op jit(solution)/shard_map/psum | solution.py:43
  509.2 21.5 %subtract_reduce_fusion = f32[16384]{0:T(1024)} fusion(f32[1024,16384]{1,0:T(8,128)} %get-tuple-element.78, f32[1024]{0:T(1024)S(1)} %get-tuple-element.126), kind=kLoop, calls=%fused_computation.15 | loop fusion | flops 33538048 | bytes 67178496 | tf_op jit(solution)/shard_map/reduce_max | solution.py:24
  530.7 3.3 all-to-all-start.6
  534.1 167.1 %while.11 = (s32[]{:T(128)}, f32[32,512]{1,0:T(8,128)S(1)}, s32[32]{0:T(128)S(1)}, s32[16384]{0:T(1024)S(1)}, f32[1024]{0:T(1024)S(1)}, /*index=5*/bf16[1024,163...) while((s32[]{:T(128)}, f32[32,512]{1,0:T(8,128)S(1)}, ...), condition=%wide.region_27.0_spmd.clone, body=%wide.region_25.27_spmd.clone.sunk | while | flops 3145226 | bytes 5308661 | solution.py:71
  537.5 1.7 fusion.19
  542.8 1.7 fusion.19
  553.2 1.7 fusion.19
  558.4 1.7 fusion.19
  568.9 1.7 fusion.19
  574.1 1.7 fusion.19
  579.3 1.7 fusion.19
  584.5 1.7 fusion.19
  701.2 24.3 %exponential_reduce_fusion = f32[16384]{0:T(1024)} fusion(f32[1024,16384]{1,0:T(8,128)} %get-tuple-element.78, f32[16384]{0:T(1024)} %subtract_reduce_fusion, f32[1024]{0:T(1024)S(1)} %get-tuple-element.166), kind=kLoop, calls=%fused_computation.8 | loop fusion | flops 50315264 | bytes 67244032 | tf_op jit(solution)/shard_map/reduce_sum | solution.py:25
  727.3 8.5 %psum.38 = f32[]{:T(128)} all-reduce(f32[]{:T(128)} %bitcast.7), channel_id=1, replica_groups=mesh['samp'=8,'state'=4] {'state'}, use_global_device_ids=true, to_apply=%region_24.0 | all-reduce | flops 1 | bytes 8 | tf_op jit(solution)/shard_map/psum | solution.py:11
  735.8 3.3 all-to-all-start.7
  740.3 2.8 all-to-all-done.7
  743.3 5.2 all_gather.15
  748.5 8.5 %all-reduce.2.cloned.1.call-done = f32[16384]{0:T(1024)} async-done(((f32[16384]{0:T(1024)}), f32[16384]{0:T(1024)}) %all-reduce.2.cloned.1.call-update) | async-done | bytes 65552 | tf_op jit(solution)/shard_map/psum | solution.py:85
  (219 shorter events, 116.5 us)
Async XLA Ops:
  104.5 28.7 %all-to-all-start = ((f32[4,1,4096]{2,1,0:T(1,128)}), f32[4,1,4096]{2,1,0:T(1,128)S(1)}, u32[]{:S(2)}, u32[]{:S(2)}) async-start(f32[4,1,4096]{2,1,0:T(1,128)} %bitcast), calls=%async_computation | async-start | bytes 131072 | tf_op jit(solution)/shard_map/all_to_all | solution.py:28
  133.2 7.4 all-to-all-start.1
  146.0 81.7 %copy-start.2 = (s32[1024]{0:T(1024)S(1)}, s32[1024]{0:T(1024)}, u32[]{:S(2)}) copy-start(s32[1024]{0:T(1024)} %param.8) | copy-start | bytes 12292
  249.2 27.7 %all-to-all-start.2 = ((f32[4,1,4096]{2,1,0:T(1,128)}), f32[4,1,4096]{2,1,0:T(1,128)S(1)}, u32[]{:S(2)}, u32[]{:S(2)}) async-start(f32[4,1,4096]{2,1,0:T(1,128)} %bitcast.2), calls=%async_computation.2 | async-start | bytes 131072 | tf_op jit(solution)/shard_map/all_to_all | solution.py:28
  276.9 7.4 all-to-all-start.3
  368.5 52.6 %copy-start.1 = (s32[16384]{0:T(1024)S(1)}, s32[16384]{0:T(1024)}, u32[]{:S(2)}) copy-start(s32[16384]{0:T(1024)} %param.9) | copy-start | bytes 196612
  390.0 27.7 %all-to-all-start.4 = ((f32[4,1,4096]{2,1,0:T(1,128)}), f32[4,1,4096]{2,1,0:T(1,128)S(1)}, u32[]{:S(2)}, u32[]{:S(2)}) async-start(f32[4,1,4096]{2,1,0:T(1,128)} %bitcast.4), calls=%async_computation.4 | async-start | bytes 131072 | tf_op jit(solution)/shard_map/all_to_all | solution.py:28
  417.8 7.4 all-to-all-start.5
  470.7 63.4 %copy-start = (f32[1024,128]{1,0:T(8,128)S(1)}, f32[1024,128]{1,0:T(8,128)}, u32[]{:S(2)}) copy-start(f32[1024,128]{1,0:T(8,128)} %param.7) | copy-start | bytes 1572868
  530.7 205.0 %all-to-all-start.6 = ((f32[4,1,4096]{2,1,0:T(1,128)}), f32[4,1,4096]{2,1,0:T(1,128)S(1)}, u32[]{:S(2)}, u32[]{:S(2)}) async-start(f32[4,1,4096]{2,1,0:T(1,128)} %bitcast.8), calls=%async_computation.6 | async-start | bytes 131072 | tf_op jit(solution)/shard_map/all_to_all | solution.py:28
  534.0 223.0 %all-reduce.2.cloned.1.call-start = ((), (), s32[]{:S(2)}) async-start(), calls=%async_computation.8 | async-start | bytes 131072 | tf_op jit(solution)/shard_map/psum | solution.py:85
  735.8 7.4 all-to-all-start.7
Sparse Core Ops, SparseCore 0:
  726.3 30.6 all-reduce.1
where the time goes:
time: 768 us; the launch traced here: 765 us
  other arithmetic  423 us (55%)
  blocking collectives  141 us (18%)
  local copies, waits for them, and re-layouts  93.4 us (12%)
  loops' own time  42.3 us (6%)
  starting transfers between devices  27.3 us (4%)
  waiting for transfers between devices  23.3 us (3%)
  between operations  14.9 us (2%)
    reduce_max x4, other arithmetic, sample_denominator(): best = jnp.max(terms, axis=0)  139 us
    reduce_sum x4, other arithmetic, sample_denominator(): total = jnp.sum(jnp.exp(terms - best[None, :]), axis=0)  97.6 us
    reduce_sum x3, other arithmetic, state_update(): total = lax.psum(jnp.sum(jnp.exp(terms - best[:, None]), axis=1), 'samp')  64.2 us
    reduce_max x3, other arithmetic, state_update(): best = lax.pmax(jnp.max(terms, axis=1), 'samp')  63 us
    pmax x3, blocking collectives, state_update(): best = lax.pmax(jnp.max(terms, axis=1), 'samp')  60.6 us
    reduce_sum x32, other arithmetic, one(): return jnp.sum(jnp.where(match, lead[:, None] - energy_part, 0.0), axis=0)  54.7 us
    psum x3, blocking collectives, state_update(): total = lax.psum(jnp.sum(jnp.exp(terms - best[:, None]), axis=1), 'samp')  51.4 us
    another operation x1, loops' own time, own_terms_local(): return lax.map(one, jnp.arange(steps_count, dtype=jnp.int32)).reshape(width)  42.3 us
  transfers between devices with their start and end apart: 9, of which 5 were waited for; matrix products, arithmetic and copies ran while one was open for 29% of the time, Pallas kernels for 0%

commit v1 on v0

--- a/solution.py
+++ b/solution.py
@@ -40,7 +40,9 @@
 def state_update(energies, offsets, denom):
     terms = -local_energy(energies, offsets) - denom[None, :]
     best = lax.pmax(jnp.max(terms, axis=1), "samp")
-    total = lax.psum(jnp.sum(jnp.exp(terms - best[:, None]), axis=1), "samp")
+    part_2 = jnp.sum(jnp.exp(terms - best[:, None]), axis=1)
+    pieces = lax.all_gather(part_2, "samp", axis=0, tiled=False)
+    total = pieces.sum(axis=0)
     return -(best + jnp.log(total))
 
 

time: 768 us -> 805 us (1.048)
  blocking collectives: 141 us -> 180 us
    all_gather x0 -> x3, blocking collectives: none -> 91.8 us  [state_update(): pieces = lax.all_gather(part_2, 'samp', axis=0, tiled=False)]
    psum x3 -> x0, blocking collectives: 51.4 us -> none  [state_update(): total = lax.psum(jnp.sum(jnp.exp(terms - best[:, None]), axis=1), 'samp')]
    reduce_sum x3 -> x6, other arithmetic: 64.2 us -> 64.2 us  [the longest x3 64.2 us: state_update(): part_2 = jnp.sum(jnp.exp(terms - best[:, None]), axis=1)]
  transfers between devices with their start and end apart: 9 -> 9, of which waited for: 5 -> 5; matrix products, arithmetic and copies ran while one was open for 29% -> 28% of each run, Pallas kernels for 0% -> 0%
where the time goes in v1:
time: 805 us; the launch traced here: 802 us
  other arithmetic  423 us (53%)
  blocking collectives  180 us (22%)
  local copies, waits for them, and re-layouts  93.4 us (12%)
  loops' own time  42.3 us (5%)
  starting transfers between devices  27.3 us (3%)
  waiting for transfers between devices  21.9 us (3%)
  between operations  14.9 us (2%)
    reduce_max x4, other arithmetic, sample_denominator(): best = jnp.max(terms, axis=0)  139 us
    reduce_sum x4, other arithmetic, sample_denominator(): total = jnp.sum(jnp.exp(terms - best[None, :]), axis=0)  97.6 us
    all_gather x3, blocking collectives, state_update(): pieces = lax.all_gather(part_2, 'samp', axis=0, tiled=False)  91.8 us
    reduce_sum x3, other arithmetic, state_update(): part_2 = jnp.sum(jnp.exp(terms - best[:, None]), axis=1)  64.2 us
    reduce_max x3, other arithmetic, state_update(): best = lax.pmax(jnp.max(terms, axis=1), 'samp')  63 us
    pmax x3, blocking collectives, state_update(): best = lax.pmax(jnp.max(terms, axis=1), 'samp')  58.6 us
    reduce_sum x32, other arithmetic, one(): return jnp.sum(jnp.where(match, lead[:, None] - energy_part, 0.0), axis=0)  54.7 us
    another operation x1, loops' own time, own_terms_local(): return lax.map(one, jnp.arange(steps_count, dtype=jnp.int32)).reshape(width)  42.3 us
  transfers between devices with their start and end apart: 9, of which 5 were waited for; matrix products, arithmetic and copies ran while one was open for 28% of the time, Pallas kernels for 0%

profile of v1, /device:TPU:0, one launch (start us, length us, event | category | flops | bytes accessed | tf_op | source)
XLA Modules:
  0.0 802.4 jit_solution(3402016208443005677)
XLA Ops:
  7.9 22.2 %add.42 = f32[1024,128,128]{2,1,0:T(8,128)} broadcast(f32[1024,128]{1,0:T(8,128)} %param.7), dimensions={0,1} | broadcast | bytes 67633152 | tf_op jit(solution)/shard_map/add | solution.py:18
  30.0 74.5 %subtract_reduce_fusion.6 = (f32[16384]{0:T(1024)}, f32[1024,16384]{1,0:T(8,128)}) fusion(f32[1024]{0:T(1024)S(1)} %convert_log_fusion, f32[128,8,128,128]{3,2,1,0:T(8,128)} %bitcast.23, bf16[1024,16384]{1,0:T(8,128)(2,1)} %param.6), kind=kLoop, calls=%fused_computation.21 | loop fusion | flops 67092480 | bytes 167841792 | tf_op jit(solution)/shard_map/reduce_max | solution.py:24
  104.5 4.3 all-to-all-start
  108.8 24.4 %exponential_reduce_fusion.6 = f32[16384]{0:T(1024)} fusion(f32[1024,16384]{1,0:T(8,128)} %get-tuple-element.78, f32[16384]{0:T(1024)} %get-tuple-element.77, f32[1024]{0:T(1024)S(1)} %convert_log_fusion), kind=kLoop, calls=%fused_computation.14 | loop fusion | flops 50315264 | bytes 67244032 | tf_op jit(solution)/shard_map/reduce_sum | solution.py:25
  133.2 3.3 all-to-all-start.1
  136.6 4.1 all-to-all-done.1
  140.7 5.2 all_gather.30
  146.0 21.0 %subtract_reduce_fusion.5 = f32[1024]{0:T(1024)S(1)} fusion(f32[1024,16384]{1,0:T(8,128)} %get-tuple-element.78, f32[16384]{0:T(1024)S(1)} %all_gather.30), kind=kLoop, calls=%fused_computation.20 | loop fusion | flops 50330624 | bytes 67178496 | tf_op jit(solution)/shard_map/reduce_max | solution.py:42
  167.0 22.1 %pmax.21 = f32[1024]{0:T(1024)S(1)} all-reduce(f32[1024]{0:T(1024)S(1)} %subtract_reduce_fusion.5), channel_id=1, replica_groups=mesh['samp'=8,'state'=4] {'samp'}, use_global_device_ids=true, to_apply=%region_5.0 | all-reduce | flops 1024 | bytes 8192 | tf_op jit(solution)/shard_map/pmax | solution.py:42
  189.1 21.4 %exponential_reduce_fusion.5 = f32[1024]{0:T(1024)S(1)} fusion(f32[1024,16384]{1,0:T(8,128)} %get-tuple-element.78, f32[1024]{0:T(1024)S(1)} %pmax.21, f32[16384]{0:T(1024)S(1)} %all_gather.30), kind=kLoop, calls=%fused_computation.13 | loop fusion | flops 67107840 | bytes 67182592 | tf_op jit(solution)/shard_map/reduce_sum | solution.py:43
  210.5 30.6 %all-gather = f32[8192]{0:T(1024)S(1)} all-gather(f32[1024]{0:T(1024)S(1)} %exponential_reduce_fusion.5), channel_id=2, replica_groups=mesh['samp'=8,'state'=4] {'samp'}, dimensions={0}, use_global_device_ids=true | all-gather | bytes 36864 | tf_op jit(solution)/shard_map/all_gather | solution.py:44
  241.2 21.5 %subtract_reduce_fusion.4 = f32[16384]{0:T(1024)} fusion(f32[1024,16384]{1,0:T(8,128)} %get-tuple-element.78, f32[1024]{0:T(1024)S(1)} %negate_add_fusion.1), kind=kLoop, calls=%fused_computation.19 | loop fusion | flops 33538048 | bytes 67178496 | tf_op jit(solution)/shard_map/reduce_max | solution.py:24
  262.7 3.3 all-to-all-start.2
  266.0 24.4 %exponential_reduce_fusion.4 = f32[16384]{0:T(1024)} fusion(f32[1024,16384]{1,0:T(8,128)} %get-tuple-element.78, f32[16384]{0:T(1024)} %subtract_reduce_fusion.4, f32[1024]{0:T(1024)S(1)} %negate_add_fusion.1), kind=kLoop, calls=%fused_computation.12 | loop fusion | flops 50315264 | bytes 67244032 | tf_op jit(solution)/shard_map/reduce_sum | solution.py:25
  290.4 3.3 all-to-all-start.3
  293.8 4.0 all-to-all-done.3
  297.9 5.2 all_gather.33
  303.2 21.0 %subtract_reduce_fusion.3 = f32[1024]{0:T(1024)S(1)} fusion(f32[1024,16384]{1,0:T(8,128)} %get-tuple-element.78, f32[16384]{0:T(1024)S(1)} %all_gather.33), kind=kLoop, calls=%fused_computation.18 | loop fusion | flops 50330624 | bytes 67178496 | tf_op jit(solution)/shard_map/reduce_max | solution.py:42
  324.2 17.3 %pmax.22 = f32[1024]{0:T(1024)S(1)} all-reduce(f32[1024]{0:T(1024)S(1)} %subtract_reduce_fusion.3), channel_id=1, replica_groups=mesh['samp'=8,'state'=4] {'samp'}, use_global_device_ids=true, to_apply=%region_13.0 | all-reduce | flops 1024 | bytes 8192 | tf_op jit(solution)/shard_map/pmax | solution.py:42
  341.5 21.4 %exponential_reduce_fusion.3 = f32[1024]{0:T(1024)S(1)} fusion(f32[1024,16384]{1,0:T(8,128)} %get-tuple-element.78, f32[1024]{0:T(1024)S(1)} %pmax.22, f32[16384]{0:T(1024)S(1)} %all_gather.33), kind=kLoop, calls=%fused_computation.11 | loop fusion | flops 67107840 | bytes 67182592 | tf_op jit(solution)/shard_map/reduce_sum | solution.py:43
  362.9 30.6 %all-gather.1 = f32[8192]{0:T(1024)S(1)} all-gather(f32[1024]{0:T(1024)S(1)} %exponential_reduce_fusion.3), channel_id=3, replica_groups=mesh['samp'=8,'state'=4] {'samp'}, dimensions={0}, use_global_device_ids=true | all-gather | bytes 36864 | tf_op jit(solution)/shard_map/all_gather | solution.py:44
  393.5 21.5 %subtract_reduce_fusion.2 = f32[16384]{0:T(1024)} fusion(f32[1024,16384]{1,0:T(8,128)} %get-tuple-element.78, f32[1024]{0:T(1024)S(1)} %negate_add_fusion), kind=kLoop, calls=%fused_computation.17 | loop fusion | flops 33538048 | bytes 67178496 | tf_op jit(solution)/shard_map/reduce_max | solution.py:24
  415.0 3.3 all-to-all-start.4
  418.3 24.4 %exponential_reduce_fusion.2 = f32[16384]{0:T(1024)} fusion(f32[1024,16384]{1,0:T(8,128)} %get-tuple-element.78, f32[16384]{0:T(1024)} %subtract_reduce_fusion.2, f32[1024]{0:T(1024)S(1)} %negate_add_fusion), kind=kLoop, calls=%fused_computation.10 | loop fusion | flops 50315264 | bytes 67244032 | tf_op jit(solution)/shard_map/reduce_sum | solution.py:25
  442.8 3.3 all-to-all-start.5
  446.2 4.0 all-to-all-done.5
  450.3 5.2 all_gather.36
  455.5 21.0 %subtract_reduce_fusion.1 = f32[1024]{0:T(1024)S(1)} fusion(f32[1024,16384]{1,0:T(8,128)} %get-tuple-element.78, f32[16384]{0:T(1024)S(1)} %all_gather.36), kind=kLoop, calls=%fused_computation.16 | loop fusion | flops 50330624 | bytes 67178496 | tf_op jit(solution)/shard_map/reduce_max | solution.py:42
  476.5 19.1 %pmax.23 = f32[1024]{0:T(1024)S(1)} all-reduce(f32[1024]{0:T(1024)S(1)} %subtract_reduce_fusion.1), channel_id=1, replica_groups=mesh['samp'=8,'state'=4] {'samp'}, use_global_device_ids=true, to_apply=%region_21.0 | all-reduce | flops 1024 | bytes 8192 | tf_op jit(solution)/shard_map/pmax | solution.py:42
  495.7 21.4 %exponential_reduce_fusion.1 = f32[1024]{0:T(1024)S(1)} fusion(f32[1024,16384]{1,0:T(8,128)} %get-tuple-element.78, f32[1024]{0:T(1024)S(1)} %pmax.23, f32[16384]{0:T(1024)S(1)} %all_gather.36), kind=kLoop, calls=%fused_computation.9 | loop fusion | flops 67107840 | bytes 67182592 | tf_op jit(solution)/shard_map/reduce_sum | solution.py:43
  517.1 30.6 %all-gather.2 = f32[8192]{0:T(1024)S(1)} all-gather(f32[1024]{0:T(1024)S(1)} %exponential_reduce_fusion.1), channel_id=4, replica_groups=mesh['samp'=8,'state'=4] {'samp'}, dimensions={0}, use_global_device_ids=true | all-gather | bytes 36864 | tf_op jit(solution)/shard_map/all_gather | solution.py:44
  547.8 21.5 %subtract_reduce_fusion = f32[16384]{0:T(1024)} fusion(f32[1024,16384]{1,0:T(8,128)} %get-tuple-element.78, f32[1024]{0:T(1024)S(1)} %get-tuple-element.126), kind=kLoop, calls=%fused_computation.15 | loop fusion | flops 33538048 | bytes 67178496 | tf_op jit(solution)/shard_map/reduce_max | solution.py:24
  569.3 3.3 all-to-all-start.6
  572.6 167.0 %while.11 = (s32[]{:T(128)}, f32[32,512]{1,0:T(8,128)S(1)}, s32[32]{0:T(128)S(1)}, s32[16384]{0:T(1024)S(1)}, f32[1024]{0:T(1024)S(1)}, /*index=5*/bf16[1024,163...) while((s32[]{:T(128)}, f32[32,512]{1,0:T(8,128)S(1)}, ...), condition=%wide.region_27.0_spmd.clone, body=%wide.region_25.27_spmd.clone.sunk | while | flops 3145226 | bytes 5308661 | solution.py:73
  576.1 1.7 fusion.19
  586.5 1.7 fusion.19
  591.7 1.7 fusion.19
  602.2 1.7 fusion.19
  607.4 1.7 fusion.19
  617.8 1.7 fusion.19
  623.0 1.7 fusion.19
  633.5 1.7 fusion.19
  739.7 24.3 %exponential_reduce_fusion = f32[16384]{0:T(1024)} fusion(f32[1024,16384]{1,0:T(8,128)} %get-tuple-element.78, f32[16384]{0:T(1024)} %subtract_reduce_fusion, f32[1024]{0:T(1024)S(1)} %get-tuple-element.166), kind=kLoop, calls=%fused_computation.8 | loop fusion | flops 50315264 | bytes 67244032 | tf_op jit(solution)/shard_map/reduce_sum | solution.py:25
  765.8 8.5 %psum.14 = f32[]{:T(128)} all-reduce(f32[]{:T(128)} %bitcast.7), channel_id=1, replica_groups=mesh['samp'=8,'state'=4] {'state'}, use_global_device_ids=true, to_apply=%region_24.0 | all-reduce | flops 1 | bytes 8 | tf_op jit(solution)/shard_map/psum | solution.py:11
  774.3 3.3 all-to-all-start.7
  778.8 2.8 all-to-all-done.7
  781.8 5.2 all_gather.39
  787.0 7.0 all-reduce.2.cloned.1.call-done
  (225 shorter events, 116.5 us)
Async XLA Ops:
  104.5 28.7 %all-to-all-start = ((f32[4,1,4096]{2,1,0:T(1,128)}), f32[4,1,4096]{2,1,0:T(1,128)S(1)}, u32[]{:S(2)}, u32[]{:S(2)}) async-start(f32[4,1,4096]{2,1,0:T(1,128)} %bitcast), calls=%async_computation | async-start | bytes 131072 | tf_op jit(solution)/shard_map/all_to_all | solution.py:28
  133.2 7.4 all-to-all-start.1
  146.0 95.2 %copy-start.2 = (s32[1024]{0:T(1024)S(1)}, s32[1024]{0:T(1024)}, u32[]{:S(2)}) copy-start(s32[1024]{0:T(1024)} %param.8) | copy-start | bytes 12292
  262.7 27.7 %all-to-all-start.2 = ((f32[4,1,4096]{2,1,0:T(1,128)}), f32[4,1,4096]{2,1,0:T(1,128)S(1)}, u32[]{:S(2)}, u32[]{:S(2)}) async-start(f32[4,1,4096]{2,1,0:T(1,128)} %bitcast.2), calls=%async_computation.2 | async-start | bytes 131072 | tf_op jit(solution)/shard_map/all_to_all | solution.py:28
  290.4 7.4 all-to-all-start.3
  393.5 52.6 %copy-start.1 = (s32[16384]{0:T(1024)S(1)}, s32[16384]{0:T(1024)}, u32[]{:S(2)}) copy-start(s32[16384]{0:T(1024)} %param.9) | copy-start | bytes 196612
  415.0 27.7 %all-to-all-start.4 = ((f32[4,1,4096]{2,1,0:T(1,128)}), f32[4,1,4096]{2,1,0:T(1,128)S(1)}, u32[]{:S(2)}, u32[]{:S(2)}) async-start(f32[4,1,4096]{2,1,0:T(1,128)} %bitcast.4), calls=%async_computation.4 | async-start | bytes 131072 | tf_op jit(solution)/shard_map/all_to_all | solution.py:28
  442.8 7.4 all-to-all-start.5
  495.7 76.9 %copy-start = (f32[1024,128]{1,0:T(8,128)S(1)}, f32[1024,128]{1,0:T(8,128)}, u32[]{:S(2)}) copy-start(f32[1024,128]{1,0:T(8,128)} %param.7) | copy-start | bytes 1572868
  569.3 205.0 %all-to-all-start.6 = ((f32[4,1,4096]{2,1,0:T(1,128)}), f32[4,1,4096]{2,1,0:T(1,128)S(1)}, u32[]{:S(2)}, u32[]{:S(2)}) async-start(f32[4,1,4096]{2,1,0:T(1,128)} %bitcast.8), calls=%async_computation.6 | async-start | bytes 131072 | tf_op jit(solution)/shard_map/all_to_all | solution.py:28
  572.6 221.5 %all-reduce.2.cloned.1.call-start = ((), (), s32[]{:S(2)}) async-start(), calls=%async_computation.8 | async-start | bytes 131072 | tf_op jit(solution)/shard_map/psum | solution.py:87
  774.3 7.4 all-to-all-start.7
Sparse Core Ops, SparseCore 0:
  764.8 29.2 all-reduce.1
